TPU v7x, 512 devices: a whole 4x8x8 slice. The times are simulated.
512 devices in a mesh: dp: 128 (over y, z, core), term: 4 (over x).
Axes of the slice: x: 4, y: 8, z: 8, core: 2. Of those that a mesh axis runs over, the one named last changes fastest.
Arguments:
- hidden: bfloat16 [128, 256, 768], P('dp'), may hold values from -100 to 100, as said below
- segment_ids: int32 [128, 256], replicated, may hold values from 0 to 3, never falling along the last dimension, each value on 1 to 160 neighbouring positions
- block_lists: int32 [512, 128], replicated, may hold values from 0 to 255, all different within a row
- doc_ids: int32 [512], replicated, may hold values from 0 to 511, each once
- attn_gain: float32 [768], replicated, may hold values from 0.1 to 1.9
- qkv_weight: bfloat16 [3, 768, 768], P(None, None, 'term'), may hold values from -0.21875 to 0.21875
- attn_out: bfloat16 [768, 768], P('term'), may hold values from -0.21875 to 0.21875
- mlp_gain: float32 [768], replicated, may hold values from 0.1 to 1.9
- ffn_in: bfloat16 [2, 768, 1152], P(None, None, 'term'), may hold values from -0.21875 to 0.21875
- ffn_out: bfloat16 [1152, 768], P('term'), may hold values from -0.1875 to 0.1875
- final_gain: float32 [768], replicated, may hold values from 0.1 to 1.9
- head_dense: bfloat16 [768, 768], replicated, may hold values from -0.21875 to 0.21875
- head_gain: float32 [768], replicated, may hold values from 0.1 to 1.9
- decoder: bfloat16 [4, 8, 128, 8, 768], P('term', None, 'dp'), may hold values from -0.21875 to 0.21875
- decoder_bias: bfloat16 [4, 8, 128, 8], P('term', None, 'dp'), may hold values from -5 to 5
Outputs:
- postings: float32 [4, 8, 128, 8, 512], P('term', None, 'dp')
Inputs may be any that keep to these rules, and one draw needn't show every extreme that they name: `hidden`: every token has its own scale, and every feature its own scale. `segment_ids`: each row's numbers never fall and each of 0 to 3 appears; a passage has 1 to 160 tokens, and some passage of each row has exactly 160. `block_lists`: a passage lists 128 different blocks; every block is listed by some passage. `doc_ids`: each column appears once.
All inputs are finite; a program needn't handle non-finite values.
Results may differ from a plain program's by a relative error of at most 0.0035.
Values may be sent and summed in bfloat16 or wider, within the bound.
No kernel may reach another device: no remote copies, remote signals or barrier semaphores. Data moves between devices by JAX's collectives and lax.ppermute only.
A program may use at most 128 MiB of HBM per device.

v0:
```python
import jax
import jax.numpy as jnp
from jax import lax
from jax.sharding import PartitionSpec as P

BLOCK = 128
HALF_WIN = 64
PASS_DEV = 4
HEAD_DIM = 64


def layer_norm(values, gain_vec):
    average = jnp.mean(values, axis=-1, keepdims=True)
    centered = values - average
    spread = jnp.mean(centered * centered, axis=-1, keepdims=True)
    return centered * lax.rsqrt(spread + 1e-05) * gain_vec


def rotary(values, positions):
    half_dim = values.shape[-1] // 2
    frequency = 10000.0 ** (-2.0 * jnp.arange(half_dim, dtype=jnp.float32) / values.shape[-1])
    angles = positions.astype(jnp.float32)[:, None] * frequency[None, :]
    cosine = jnp.cos(angles)[:, None, :]
    sine_part = jnp.sin(angles)[:, None, :]
    first_half = values[..., :half_dim]
    second = values[..., half_dim:]
    return jnp.concatenate(
        [first_half * cosine - second * sine_part, second * cosine + first_half * sine_part],
        axis=-1,
    )


def head_block(residual, final_gain, head_dense, head_gain):
    normed_out = layer_norm(residual, final_gain).astype(jnp.bfloat16)
    dense_out = jnp.dot(normed_out, head_dense, preferred_element_type=jnp.float32)
    return layer_norm(jax.nn.gelu(dense_out, approximate=False), head_gain).astype(jnp.bfloat16)


def passage_maxima(activity, segments):
    return jnp.stack(
        [
            jnp.max(jnp.where(segments[..., None] == passage, activity, 0.0), axis=-2)
            for passage in range(PASS_DEV)
        ],
        axis=-2,
    )


def on_device(
    hidden,
    segment_ids,
    block_lists,
    doc_ids,
    attn_gain,
    qkv_weight,
    attn_out,
    mlp_gain,
    ffn_in,
    ffn_out,
    final_gain,
    head_dense,
    head_gain,
    decoder,
    decoder_bias,
):
    row_index = lax.axis_index("dp")
    dp_count = lax.axis_size("dp")
    tokens = hidden[0]
    length = tokens.shape[0]
    width = tokens.shape[1]
    segments = lax.dynamic_index_in_dim(segment_ids, row_index, 0, keepdims=False)
    token_index = jnp.arange(length, dtype=jnp.int32)
    positions = token_index - jnp.sum(
        (segments[None, :] < segments[:, None]).astype(jnp.int32), axis=1
    )
    allowed = (segments[:, None] == segments[None, :]) & (
        jnp.abs(token_index[:, None] - token_index[None, :]) <= HALF_WIN
    )
    normed = layer_norm(tokens.astype(jnp.float32), attn_gain).astype(jnp.bfloat16)
    head_width = qkv_weight.shape[2]
    local_heads = head_width // HEAD_DIM

    def project(which_slot):
        return jnp.dot(normed, qkv_weight[which_slot], preferred_element_type=jnp.float32).reshape(
            length, local_heads, HEAD_DIM
        )

    queries = rotary(project(0), positions).astype(jnp.bfloat16)
    key_rows = rotary(project(1), positions).astype(jnp.bfloat16)
    values = project(2).astype(jnp.bfloat16)
    scores = jnp.einsum(
        "qhd,khd->hqk", queries, key_rows, preferred_element_type=jnp.float32
    ) * HEAD_DIM ** (-0.5)
    raised = jnp.where(allowed[None], jnp.exp(scores), 0.0)
    probabilities = (raised / jnp.sum(raised, axis=-1, keepdims=True)).astype(jnp.bfloat16)
    context = jnp.einsum("hqk,khd->qhd", probabilities, values, preferred_element_type=jnp.float32)
    context = context.astype(jnp.bfloat16).reshape(length, head_width)
    partial_attn = jnp.dot(context, attn_out, preferred_element_type=jnp.float32)
    after_attn = tokens.astype(jnp.float32) + lax.psum(partial_attn, "term")
    mixed_in = layer_norm(after_attn, mlp_gain).astype(jnp.bfloat16)
    inner_up = jnp.dot(mixed_in, ffn_in[0], preferred_element_type=jnp.float32)
    gate_part = jnp.dot(mixed_in, ffn_in[1], preferred_element_type=jnp.float32)
    activated = (jax.nn.gelu(inner_up, approximate=False) * gate_part).astype(jnp.bfloat16)
    partial_ffn = jnp.dot(activated, ffn_out, preferred_element_type=jnp.float32)
    summed = lax.psum(partial_ffn, "term")
    headed = head_block(after_attn + summed, final_gain, head_dense, head_gain)
    groups = decoder.shape[1]
    span = decoder.shape[3]
    part_terms = dp_count * span
    range_width = groups * part_terms
    range_start = lax.axis_index("term") * range_width
    passages = block_lists.shape[0]
    rows_weight = lax.all_gather(decoder, "dp", axis=2, tiled=True)
    rows_bias = lax.all_gather(decoder_bias, "dp", axis=2, tiled=True)
    count = rows_weight.shape[2]
    flat_rows = rows_weight[0].reshape(groups * count * span, width)
    logits = lax.dot_general(
        headed, flat_rows, (((1,), (1,)), ((), ())), preferred_element_type=jnp.float32
    )
    logits = logits + rows_bias[0].reshape(groups * count * span).astype(jnp.float32)[None, :]
    activity = jnp.log1p(jnp.maximum(logits, 0.0))
    maxima = passage_maxima(activity, segments).reshape(PASS_DEV, groups, count, span)
    term_order = jnp.arange(range_width, dtype=jnp.int32)
    term_blocks = (range_start + term_order) // BLOCK
    own_lists = lax.dynamic_slice_in_dim(block_lists, row_index * PASS_DEV, PASS_DEV, 0)
    listed = jnp.any(own_lists[:, :, None] == term_blocks[None, None, :], axis=1).astype(
        jnp.float32
    )
    weighted = maxima * listed.reshape(PASS_DEV, groups, dp_count, span)
    received = lax.all_to_all(weighted, "dp", split_axis=2, concat_axis=0, tiled=True)
    own_weights = received[:, :, 0, :]
    placed = (
        jnp.zeros((groups, span, passages), jnp.float32)
        .at[:, :, doc_ids]
        .set(jnp.transpose(own_weights, (1, 2, 0)))
    )
    return placed[None, :, None]


def solution(mesh):
    in_specs = (
        P("dp", None, None),
        P(),
        P(),
        P(),
        P(),
        P(None, None, "term"),
        P("term", None),
        P(),
        P(None, None, "term"),
        P("term", None),
        P(),
        P(),
        P(),
        P("term", None, "dp", None, None),
        P("term", None, "dp", None),
    )
    out_specs = P("term", None, "dp", None, None)
    return jax.shard_map(
        on_device, mesh=mesh, in_specs=in_specs, out_specs=out_specs, check_vma=False
    )
```

profile of v0, /device:TPU:1, one launch (start us, length us, event | category | flops | bytes accessed | tf_op | source)
XLA Modules:
  0.0 268.6 jit_solution(5582998730450174788)
XLA Ops:
  7.4 0.0 copy-start
  7.4 0.0 all-reduce.3.cloned.1.call-start
  7.4 0.8 constant_dynamic-slice_fusion
  8.2 0.1 convert_reduce_fusion.1
  8.3 0.1 fusion.97
  8.5 1.1 convert_reduce_fusion
  9.6 1.2 fusion.9
  10.9 1.2 fusion.182
  12.1 0.2 fusion.30
  12.3 0.3 fusion.184
  12.6 0.3 fusion.185
  12.9 0.2 multiply_cosine_fusion
  13.1 0.1 subtract_convert_fusion
  13.2 0.0 copy-start.3
  13.2 1.2 fusion.3
  14.4 1.8 convolution_convert_fusion
  16.2 0.0 copy-done.3
  16.2 0.0 copy-start.5
  16.2 1.2 fusion.186
  17.4 0.0 all-reduce.3.cloned.1.call-update
  17.5 0.0 all-reduce.5.cloned.1.call-start
  17.5 58.9 %all-reduce.3.cloned.1.call-done = f32[256,768]{1,0:T(8,128)} async-done(((f32[256,768]{1,0:T(8,128)}), f32[256,768]{1,0:T(8,128)}) %all-reduce.3.cloned.1.call-update) | async-done | bytes 786448 | tf_op jit(solution)/shard_map/psum | solution.py:99
  76.4 1.4 fusion.140
  77.7 0.0 copy-start.8
  77.8 1.4 multiply_reduce_fusion.2
  79.2 0.2 multiply_convert_fusion.2
  79.4 1.3 fusion.24
  80.7 0.0 copy-start.6
  80.7 3.3 %fusion.5 = f32[256,768]{1,0:T(8,128)} fusion(bf16[288,768]{1,0:T(8,128)(2,1)S(1)} %copy-done.8, bf16[256,768]{1,0:T(8,128)(2,1)S(1)} %multiply_convert_fusion.2, bf16[2,768,288]{1,2,0:T(8,128)(2,1)} %param.23, f32[256,288]{0,1:T(8,128)S(1)} %fusion.24), kind=kOutput, calls=%fused_computation.19 | convolution fusion | flops 231358464 | bytes 2359296 | tf_op jit(solution)/shard_map/dot_general | solution.py:104
  84.0 0.0 all-reduce.5.cloned.1.call-update
  84.0 0.0 all-gather.2.cloned.1.call-start
  84.1 0.5 all-gather.2.cloned.1.call-update
  84.6 53.9 %all_gather.7 = bf16[1,8,128,8]{3,1,0,2:T(8,128)(2,1)S(1)} all-gather(bf16[1,8,1,8]{3,1,0,2:T(8,128)(2,1)S(1)} %bitcast.86), channel_id=1, replica_groups=mesh['dp'=128,'term'=4] {'dp'}, dimensions={2}, use_global_device_ids=true | all-gather | bytes 16512 | tf_op jit(solution)/shard_map/all_gather | solution.py:114
  138.5 0.2 copy.42
  138.7 0.1 copy.43
  138.9 0.3 reshape.297
  139.1 0.7 constant_dynamic-slice_fusion.1
  139.9 0.0 copy-start.9
  139.9 2.6 compare_reduce_fusion
  142.5 1.3 reduce_or.12
  143.8 0.0 all-reduce.5.cloned.1.call-done
  143.8 1.3 fusion.180
  145.1 0.2 multiply_reduce_fusion.1
  145.4 0.0 copy-start.10
  145.4 2.1 fusion.183
  147.6 0.2 multiply_reduce_fusion
  147.8 36.3 %all-gather.2.cloned.1.call-done = bf16[1,8,128,8,768]{4,3,2,1,0:T(8,128)(2,1)} async-done(((bf16[1,8,1,8,768]{4,3,2,1,0:T(8,128)(2,1)}), bf16[1,8,128,8,768]{4,3,2,1,0:T(8,128)(2,1)}) %all-gather.2.cloned.1.call-update) | async-done | bytes 12582928 | tf_op jit(solution)/shard_map/all_gather | solution.py:113
  184.2 10.7 %select_reduce_fusion.3 = (f32[8192]{0:T(1024)S(1)}, f32[8192]{0:T(1024)S(1)}, f32[8192]{0:T(1024)S(1)}, f32[8192]{0:T(1024)S(1)}) fusion(pred[256]{0:T(512)(128)(4,1)S(1)} %get-tuple-element.25, pred[256]{0:T(512)(128)(4,1)S(1)} %get-tuple-element.23, pred[256]{0:T(512)(128)(4,1)S(1)} %get-tuple-element.24, pred[256]{0:T(512)(128)(4,1)S(1)} %get-tuple-element.22, ...), kind=kOutput, calls=%fused_computation.8 | convolution fusion | flops 3242950656 | bytes 13539328 | tf_op jit(solution)/shard_map/dot_general | solution.py:117
  194.9 0.3 stack.15
  195.2 0.3 stack.16
  195.5 0.3 stack.17
  195.8 1.1 stack.18
  196.9 1.4 maximum_select_fusion
  198.2 1.2 copy.48
  199.4 0.0 copy-start.7
  199.5 1.7 reshape.308
  201.2 9.3 %all-to-all-start = ((f32[128,1,256]{2,1,0:T(1,128)}), f32[128,1,256]{2,1,0:T(1,128)S(1)}, u32[]{:S(2)}, u32[]{:S(2)}) async-start(f32[128,1,256]{2,1,0:T(1,128)} %reshape.308), calls=%async_computation | async-start | bytes 262144 | tf_op jit(solution)/shard_map/all_to_all | solution.py:130
  210.5 12.2 %all-to-all-done = f32[128,1,256]{2,1,0:T(1,128)S(1)} async-done(((f32[128,1,256]{2,1,0:T(1,128)}), f32[128,1,256]{2,1,0:T(1,128)S(1)}, u32[]{:S(2)}, u32[]{:S(2)}) %all-to-all-start) | async-done | bytes 131104 | tf_op jit(solution)/shard_map/all_to_all | solution.py:130
  222.7 0.5 broadcast.282
  223.2 1.0 reduce.1
  224.1 2.5 reshape.309
  226.6 0.1 broadcast_in_dim.48
  226.8 33.1 %scatter_fusion = f32[8,8,512]{1,0,2:T(8,128)S(1)} fusion(f32[8,8,512]{1,0,2:T(8,128)S(1)} %broadcast_in_dim.48, s32[512]{0:T(512)S(1)} %compare_select_fusion, f32[512,8,8]{2,1,0:T(8,128)} %bitcast.77), kind=kCustom, calls=%fused_computation | custom fusion | bytes 395264 | tf_op jit(solution)/shard_map/scatter | solution.py:135
  259.9 1.3 copy.45
  (26 shorter events, 0.1 us)
Async XLA Ops:
  7.4 138.0 %copy-start = (bf16[768,768]{1,0:T(8,128)(2,1)S(1)}, bf16[768,768]{1,0:T(8,128)(2,1)}, u32[]{:S(2)}) copy-start(bf16[768,768]{1,0:T(8,128)(2,1)} %param.26) | copy-start | bytes 3538948
  7.4 4.7 %copy-start.1 = (bf16[1,256,768]{2,1,0:T(8,128)(2,1)S(1)}, bf16[1,256,768]{2,1,0:T(8,128)(2,1)}, u32[]{:S(2)}) copy-start(bf16[1,256,768]{2,1,0:T(8,128)(2,1)} %param.15) | copy-start | bytes 1179652
  7.4 4.7 %copy-start.4 = (f32[768]{0:T(1024)S(1)}, f32[768]{0:T(1024)}, u32[]{:S(2)}) copy-start(f32[768]{0:T(1024)} %param.19) | copy-start | bytes 9220
  7.4 69.0 %all-reduce.3.cloned.1.call-start = ((), (), s32[]{:S(2)}) async-start(), calls=%async_computation.1 | async-start | bytes 1572864 | tf_op jit(solution)/shard_map/psum | solution.py:99
  13.2 3.1 %copy-start.3 = (bf16[192,768]{1,0:T(8,128)(2,1)S(1)}, bf16[192,768]{1,0:T(8,128)(2,1)}, u32[]{:S(2)}) copy-start(bf16[192,768]{1,0:T(8,128)(2,1)} %param.21) | copy-start | bytes 884740
  16.2 63.0 %copy-start.5 = (f32[768]{0:T(1024)S(1)}, f32[768]{0:T(1024)}, u32[]{:S(2)}) copy-start(f32[768]{0:T(1024)} %param.22) | copy-start | bytes 9220
  17.5 126.3 %all-reduce.5.cloned.1.call-start = ((), (), s32[]{:S(2)}) async-start(), calls=%async_computation.2 | async-start | bytes 1572864 | tf_op jit(solution)/shard_map/psum | solution.py:105
  76.4 2.8 %copy-start.2 = (f32[256,768]{1,0:T(8,128)S(1)}, f32[256,768]{1,0:T(8,128)}, u32[]{:S(2)}) copy-start(f32[256,768]{1,0:T(8,128)} %all-reduce.3.cloned.1.call-done) | copy-start | bytes 2359300
  77.7 3.0 %copy-start.8 = (bf16[288,768]{1,0:T(8,128)(2,1)S(1)}, bf16[288,768]{1,0:T(8,128)(2,1)}, u32[]{:S(2)}) copy-start(bf16[288,768]{1,0:T(8,128)(2,1)} %param.24) | copy-start | bytes 1327108
  80.7 3.9 %copy-start.6 = (bf16[1,8,1,8]{3,1,2,0:T(8,128)(2,1)S(1)}, bf16[1,8,1,8]{3,1,2,0:T(8,128)(2,1)}, u32[]{:S(2)}) copy-start(bf16[1,8,1,8]{3,1,2,0:T(8,128)(2,1)} %param.29) | copy-start | bytes 388
  84.0 100.1 %all-gather.2.cloned.1.call-start = ((), (), s32[]{:S(2)}) async-start(), calls=%async_computation.3 | async-start | bytes 12681216 | tf_op jit(solution)/shard_map/all_gather | solution.py:113
  139.9 5.5 %copy-start.9 = (f32[768]{0:T(1024)S(1)}, f32[768]{0:T(1024)}, u32[]{:S(2)}) copy-start(f32[768]{0:T(1024)} %param.25) | copy-start | bytes 9220
  145.4 38.8 %copy-start.10 = (f32[768]{0:T(1024)S(1)}, f32[768]{0:T(1024)}, u32[]{:S(2)}) copy-start(f32[768]{0:T(1024)} %param.27) | copy-start | bytes 9220
  199.4 11.0 %copy-start.7 = (s32[512]{0:T(512)S(1)}, s32[512]{0:T(512)}, u32[]{:S(2)}) copy-start(s32[512]{0:T(512)} %param.18) | copy-start | bytes 6148
  201.2 21.5 %all-to-all-start = ((f32[128,1,256]{2,1,0:T(1,128)}), f32[128,1,256]{2,1,0:T(1,128)S(1)}, u32[]{:S(2)}, u32[]{:S(2)}) async-start(f32[128,1,256]{2,1,0:T(1,128)} %reshape.308), calls=%async_computation | async-start | bytes 262144 | tf_op jit(solution)/shard_map/all_to_all | solution.py:130
Sparse Core Ops, SparseCore 0:
  17.6 58.7 all-reduce.2
  84.1 56.7 all-reduce.4
Sparse Core Ops, SparseCore 1:
  87.8 96.3 all-gather.1
where the time goes:
time: 271 us; the launch traced here: 269 us
  waiting for transfers between devices  108 us (40%)
  blocking collectives  53.9 us (20%)
  local copies, waits for them, and re-layouts  47.1 us (17%)
  matrix products  22.3 us (8%)
  between operations  15.2 us (6%)
  other arithmetic  12.8 us (5%)
  starting transfers between devices  9.34 us (3%)
    psum x1, waiting for transfers between devices, on_device(): after_attn = tokens.astype(jnp.float32) + lax.psum(partial_attn, 'term')  58.9 us
    all_gather x1, blocking collectives, on_device(): rows_bias = lax.all_gather(decoder_bias, 'dp', axis=2, tiled=True)  53.9 us
    all_gather x1, waiting for transfers between devices, on_device(): rows_weight = lax.all_gather(decoder, 'dp', axis=2, tiled=True)  36.3 us
    scatter x1, local copies, waits for them, and re-layouts, on_device(): placed = jnp.zeros((groups, span, passages), jnp.float32).at[:, :, doc_id...  33.1 us
    all_to_all x1, waiting for transfers between devices, on_device(): lax.all_to_all(weighted, 'dp', split_axis=2, concat_axis=0, tiled=True)  12.2 us
    dot_general x1, matrix products, on_device(): lax.dot_general(headed, flat_rows, (((1,), (1,)), ((), ())), preferred_el...  10.7 us
    all_to_all x1, starting transfers between devices, on_device(): lax.all_to_all(weighted, 'dp', split_axis=2, concat_axis=0, tiled=True)  9.25 us
  transfers between devices with their start and end apart: 4, of which 3 were waited for; matrix products, arithmetic and copies ran while one was open for 3% of the time, Pallas kernels for 0%

commit v1 on v0

--- a/solution.py
+++ b/solution.py
@@ -2,6 +2,7 @@
 import jax.numpy as jnp
 from jax import lax
 from jax.sharding import PartitionSpec as P
+from jax.lax import all_gather
 
 BLOCK = 128
 HALF_WIN = 64
@@ -96,7 +97,8 @@
     context = jnp.einsum("hqk,khd->qhd", probabilities, values, preferred_element_type=jnp.float32)
     context = context.astype(jnp.bfloat16).reshape(length, head_width)
     partial_attn = jnp.dot(context, attn_out, preferred_element_type=jnp.float32)
-    after_attn = tokens.astype(jnp.float32) + lax.psum(partial_attn, "term")
+    pair_hubs = lambda buf: all_gather(buf, "term").sum(axis=0)
+    after_attn = tokens.astype(jnp.float32) + pair_hubs(partial_attn)
     mixed_in = layer_norm(after_attn, mlp_gain).astype(jnp.bfloat16)
     inner_up = jnp.dot(mixed_in, ffn_in[0], preferred_element_type=jnp.float32)
     gate_part = jnp.dot(mixed_in, ffn_in[1], preferred_element_type=jnp.float32)

time: 271 us -> 259 us (0.956)
  waiting for transfers between devices: 108 us -> 98.5 us
    psum x1 -> x0, waiting for transfers between devices: 58.9 us -> none  [on_device(): after_attn = tokens.astype(jnp.float32) + lax.psum(partial_attn, 'term')]
    all_gather x0 -> x1, waiting for transfers between devices: none -> 50.5 us  [on_device(): pair_hubs = lambda buf: all_gather(buf, 'term').sum(axis=0)]
  transfers between devices with their start and end apart: 4 -> 4, of which waited for: 3 -> 3; matrix products, arithmetic and copies ran while one was open for 3% -> 4% of each run, Pallas kernels for 0% -> 0%
where the time goes in v1:
time: 259 us; the launch traced here: 257 us
  waiting for transfers between devices  98.5 us (38%)
  blocking collectives  52.3 us (20%)
  local copies, waits for them, and re-layouts  47.7 us (18%)
  matrix products  21.3 us (8%)
  between operations  15.2 us (6%)
  other arithmetic  12.8 us (5%)
  starting transfers between devices  9.49 us (4%)
    all_gather x1, blocking collectives, on_device(): rows_bias = lax.all_gather(decoder_bias, 'dp', axis=2, tiled=True)  52.3 us
    all_gather x1, waiting for transfers between devices, on_device(): pair_hubs = lambda buf: all_gather(buf, 'term').sum(axis=0)  50.5 us
    all_gather x1, waiting for transfers between devices, on_device(): rows_weight = lax.all_gather(decoder, 'dp', axis=2, tiled=True)  35.3 us
    scatter x1, local copies, waits for them, and re-layouts, on_device(): placed = jnp.zeros((groups, span, passages), jnp.float32).at[:, :, doc_id...  33.1 us
    all_to_all x1, waiting for transfers between devices, on_device(): lax.all_to_all(weighted, 'dp', split_axis=2, concat_axis=0, tiled=True)  12.2 us
    dot_general x1, matrix products, on_device(): lax.dot_general(headed, flat_rows, (((1,), (1,)), ((), ())), preferred_el...  10.7 us
    all_to_all x1, starting transfers between devices, on_device(): lax.all_to_all(weighted, 'dp', split_axis=2, concat_axis=0, tiled=True)  9.4 us
  transfers between devices with their start and end apart: 4, of which 3 were waited for; matrix products, arithmetic and copies ran while one was open for 4% of the time, Pallas kernels for 0%

profile of v1, /device:TPU:1, one launch (start us, length us, event | category | flops | bytes accessed | tf_op | source)
XLA Modules:
  0.0 257.1 jit_solution(12659715370079522254)
XLA Ops:
  7.4 0.0 all-gather.6.cloned.1.call-start
  7.4 0.8 constant_dynamic-slice_fusion
  8.2 0.1 convert_reduce_fusion.1
  8.3 0.1 fusion.104
  8.5 1.1 convert_reduce_fusion
  9.6 1.2 fusion.9
  10.9 1.2 fusion.187
  12.1 0.2 fusion.35
  12.3 0.3 fusion.189
  12.6 0.3 fusion.190
  12.9 0.2 multiply_cosine_fusion
  13.1 0.1 subtract_convert_fusion
  13.2 0.0 copy-start.2
  13.2 1.2 fusion.3
  14.4 1.8 convolution_convert_fusion
  16.2 1.2 fusion.191
  17.4 0.0 all-gather.6.cloned.1.call-update
  17.4 0.0 all-reduce.2.cloned.1.call-start
  17.5 50.5 %all-gather.6.cloned.1.call-done = f32[1024,768]{1,0:T(8,128)} async-done(((f32[256,768]{1,0:T(8,128)}), f32[1024,768]{1,0:T(8,128)}) %all-gather.6.cloned.1.call-update) | async-done | bytes 3145744 | tf_op jit(solution)/shard_map/all_gather | solution.py:100
  68.0 2.2 reduce_sum.105
  70.1 0.0 copy-start.5
  70.1 0.0 copy-start.3
  70.2 0.2 fusion.45
  70.3 0.2 multiply_reduce_fusion.2
  70.6 0.3 copy-done.5
  70.8 0.2 fusion.34
  71.0 0.3 copy-done.3
  71.3 0.3 fusion.28
  71.6 0.0 copy-start.6
  71.7 3.3 %fusion.5 = f32[256,768]{1,0:T(8,128)} fusion(bf16[288,768]{1,0:T(8,128)(2,1)S(1)} %copy-done.8, bf16[256,768]{1,0:T(8,128)(2,1)S(1)} %fusion.34, bf16[2,768,288]{1,2,0:T(8,128)(2,1)} %param.23, f32[256,288]{0,1:T(8,128)S(1)} %fusion.28), kind=kOutput, calls=%fused_computation.20 | convolution fusion | flops 231358464 | bytes 2359296 | tf_op jit(solution)/shard_map/dot_general | solution.py:106
  74.9 0.0 all-reduce.2.cloned.1.call-update
  74.9 0.0 all-gather.4.cloned.1.call-start
  75.0 0.5 all-gather.4.cloned.1.call-update
  75.5 52.3 %all_gather.15 = bf16[1,8,128,8]{3,1,0,2:T(8,128)(2,1)S(1)} all-gather(bf16[1,8,1,8]{3,1,0,2:T(8,128)(2,1)S(1)} %bitcast.92), channel_id=1, replica_groups=mesh['dp'=128,'term'=4] {'dp'}, dimensions={2}, use_global_device_ids=true | all-gather | bytes 16512 | tf_op jit(solution)/shard_map/all_gather | solution.py:116
  127.8 0.2 copy.42
  128.0 0.1 copy.43
  128.1 0.3 reshape.340
  128.4 0.7 constant_dynamic-slice_fusion.1
  129.1 0.0 copy-start.9
  129.1 2.6 %compare_reduce_fusion = pred[4,8192]{1,0:T(4,128)(4,1)S(1)} fusion(s32[8192]{0:T(1024)S(1)} %add_select_fusion, s32[4,128]{1,0:T(4,128)S(1)} %constant_dynamic-slice_fusion.1), kind=kLoop, calls=%fused_computation.1 | loop fusion | flops 8355840 | bytes 67584 | tf_op jit(solution)/shard_map/reduce_or | solution.py:128
  131.8 1.3 reduce_or.12
  133.0 0.0 all-reduce.2.cloned.1.call-done
  133.1 1.5 fusion.185
  134.6 0.2 multiply_reduce_fusion.1
  134.8 2.2 fusion.188
  137.0 0.2 multiply_reduce_fusion
  137.2 35.3 %all-gather.4.cloned.1.call-done = bf16[1,8,128,8,768]{4,3,2,1,0:T(8,128)(2,1)} async-done(((bf16[1,8,1,8,768]{4,3,2,1,0:T(8,128)(2,1)}), bf16[1,8,128,8,768]{4,3,2,1,0:T(8,128)(2,1)}) %all-gather.4.cloned.1.call-update) | async-done | bytes 12582928 | tf_op jit(solution)/shard_map/all_gather | solution.py:115
  172.5 10.7 %select_reduce_fusion.3 = (f32[8192]{0:T(1024)S(1)}, f32[8192]{0:T(1024)S(1)}, f32[8192]{0:T(1024)S(1)}, f32[8192]{0:T(1024)S(1)}) fusion(pred[256]{0:T(512)(128)(4,1)S(1)} %get-tuple-element.25, pred[256]{0:T(512)(128)(4,1)S(1)} %get-tuple-element.23, pred[256]{0:T(512)(128)(4,1)S(1)} %get-tuple-element.24, pred[256]{0:T(512)(128)(4,1)S(1)} %get-tuple-element.22, ...), kind=kOutput, calls=%fused_computation.8 | convolution fusion | flops 3242950656 | bytes 13539328 | tf_op jit(solution)/shard_map/dot_general | solution.py:119
  183.2 0.3 stack.15
  183.5 0.3 stack.16
  183.8 0.3 stack.17
  184.1 1.1 stack.18
  185.2 1.4 maximum_select_fusion
  186.6 1.2 copy.48
  187.8 0.0 copy-start.7
  187.8 1.7 reshape.352
  189.6 9.4 %all-to-all-start = ((f32[128,1,256]{2,1,0:T(1,128)}), f32[128,1,256]{2,1,0:T(1,128)S(1)}, u32[]{:S(2)}, u32[]{:S(2)}) async-start(f32[128,1,256]{2,1,0:T(1,128)} %reshape.352), calls=%async_computation | async-start | bytes 262144 | tf_op jit(solution)/shard_map/all_to_all | solution.py:132
  199.0 12.2 %all-to-all-done = f32[128,1,256]{2,1,0:T(1,128)S(1)} async-done(((f32[128,1,256]{2,1,0:T(1,128)}), f32[128,1,256]{2,1,0:T(1,128)S(1)}, u32[]{:S(2)}, u32[]{:S(2)}) %all-to-all-start) | async-done | bytes 131104 | tf_op jit(solution)/shard_map/all_to_all | solution.py:132
  211.2 0.5 broadcast.303
  211.7 1.0 reduce.1
  212.6 2.5 reshape.353
  215.2 0.1 broadcast_in_dim.48
  215.3 33.1 %scatter_fusion = f32[8,8,512]{1,0,2:T(8,128)S(1)} fusion(f32[8,8,512]{1,0,2:T(8,128)S(1)} %broadcast_in_dim.48, s32[512]{0:T(512)S(1)} %compare_select_fusion, f32[512,8,8]{2,1,0:T(8,128)} %bitcast.82), kind=kCustom, calls=%fused_computation | custom fusion | bytes 395264 | tf_op jit(solution)/shard_map/scatter | solution.py:137
  248.4 1.3 copy.45
  (27 shorter events, 0.1 us)
Async XLA Ops:
  7.4 127.4 %copy-start = (bf16[768,768]{1,0:T(8,128)(2,1)S(1)}, bf16[768,768]{1,0:T(8,128)(2,1)}, u32[]{:S(2)}) copy-start(bf16[768,768]{1,0:T(8,128)(2,1)} %param.26) | copy-start | bytes 3538948
  7.4 4.7 %copy-start.1 = (bf16[1,256,768]{2,1,0:T(8,128)(2,1)S(1)}, bf16[1,256,768]{2,1,0:T(8,128)(2,1)}, u32[]{:S(2)}) copy-start(bf16[1,256,768]{2,1,0:T(8,128)(2,1)} %param.15) | copy-start | bytes 1179652
  7.4 4.7 %copy-start.4 = (f32[768]{0:T(1024)S(1)}, f32[768]{0:T(1024)}, u32[]{:S(2)}) copy-start(f32[768]{0:T(1024)} %param.19) | copy-start | bytes 9220
  7.4 60.6 %all-gather.6.cloned.1.call-start = ((), (), s32[]{:S(2)}) async-start(), calls=%async_computation.3 | async-start | bytes 3932160 | tf_op jit(solution)/shard_map/all_gather | solution.py:100
  13.2 3.1 %copy-start.2 = (bf16[192,768]{1,0:T(8,128)(2,1)S(1)}, bf16[192,768]{1,0:T(8,128)(2,1)}, u32[]{:S(2)}) copy-start(bf16[192,768]{1,0:T(8,128)(2,1)} %param.21) | copy-start | bytes 884740
  17.4 115.6 %all-reduce.2.cloned.1.call-start = ((), (), s32[]{:S(2)}) async-start(), calls=%async_computation.1 | async-start | bytes 1572864 | tf_op jit(solution)/shard_map/psum | solution.py:107
  70.1 0.7 copy-start.5
  70.1 1.2 copy-start.3
  70.3 1.3 copy-start.8
  71.6 3.9 %copy-start.6 = (bf16[1,8,1,8]{3,1,2,0:T(8,128)(2,1)S(1)}, bf16[1,8,1,8]{3,1,2,0:T(8,128)(2,1)}, u32[]{:S(2)}) copy-start(bf16[1,8,1,8]{3,1,2,0:T(8,128)(2,1)} %param.29) | copy-start | bytes 388
  74.9 97.6 %all-gather.4.cloned.1.call-start = ((), (), s32[]{:S(2)}) async-start(), calls=%async_computation.2 | async-start | bytes 12681216 | tf_op jit(solution)/shard_map/all_gather | solution.py:115
  129.1 5.7 %copy-start.9 = (f32[768]{0:T(1024)S(1)}, f32[768]{0:T(1024)}, u32[]{:S(2)}) copy-start(f32[768]{0:T(1024)} %param.25) | copy-start | bytes 9220
  134.8 37.7 %copy-start.10 = (f32[768]{0:T(1024)S(1)}, f32[768]{0:T(1024)}, u32[]{:S(2)}) copy-start(f32[768]{0:T(1024)} %param.27) | copy-start | bytes 9220
  187.8 11.1 %copy-start.7 = (s32[512]{0:T(512)S(1)}, s32[512]{0:T(512)}, u32[]{:S(2)}) copy-start(s32[512]{0:T(512)} %param.18) | copy-start | bytes 6148
  189.6 21.6 %all-to-all-start = ((f32[128,1,256]{2,1,0:T(1,128)}), f32[128,1,256]{2,1,0:T(1,128)S(1)}, u32[]{:S(2)}, u32[]{:S(2)}) async-start(f32[128,1,256]{2,1,0:T(1,128)} %reshape.352), calls=%async_computation | async-start | bytes 262144 | tf_op jit(solution)/shard_map/all_to_all | solution.py:132
Sparse Core Ops, SparseCore 0:
  17.6 50.3 all-gather.5
  75.1 54.0 all-reduce.1
Sparse Core Ops, SparseCore 1:
  78.7 93.8 all-gather.3
